TPU v7x, 512 devices: a whole 4x8x8 slice. The times are simulated.
512 devices in a mesh: dp: 32 (over y_hi, z), inblk: 4 (over x), outcol: 4 (over y_lo, core).
Axes of the slice: x: 4, y: 8 (y_hi: 4, y_lo: 2; y = y_hi * 2 + y_lo), z: 8, core: 2. Of those that a mesh axis runs over, the one named last changes fastest.
Arguments:
- activations: bfloat16 [4096, 8192], P('dp', ('inblk', 'outcol')), may hold values from -1.5 to 1.5
- cotangent: bfloat16 [4096, 1024], P('dp', 'outcol'), may hold values from -6 to 6
- base_weight: bfloat16 [8192, 1024], P('inblk', 'outcol'), may hold values from -0.09375 to 0.09375
- skew_param: float32 [32, 256, 256], P(('inblk', 'outcol'), 'dp'), may hold values from -0.3125 to 0.3125
Outputs:
- grad_acts: bfloat16 [4096, 8192], P('dp', ('inblk', 'outcol'))
- grad_skew: float32 [32, 256, 256], P(('inblk', 'outcol'), 'dp')
All inputs are finite; a program needn't handle non-finite values.
Results may differ from a plain program's by a relative error of at most 0.0058.
Values may be sent and summed in bfloat16 or wider, within the bound.
No kernel may reach another device: no remote copies, remote signals or barrier semaphores. Data moves between devices by JAX's collectives and lax.ppermute only.
A program may use at most 64 MiB of HBM per device.

v0:
```python
import jax
import jax.numpy as jnp
from jax import lax
from jax.sharding import PartitionSpec as P


def high_product(left, right):
    return jnp.matmul(left, right, precision=lax.Precision.HIGHEST)


def power_list(skew_input):
    skew_mat = skew_input - jnp.swapaxes(skew_input, -1, -2)
    powers = [skew_mat]
    for degree in range(5):
        powers.append(high_product(powers[-1], skew_mat))
    return powers


def rotation_of(powers):
    block_width = powers[0].shape[-1]
    identity_mat = jnp.eye(block_width, dtype=jnp.float32)
    series = powers[0] + powers[1] + powers[2] + powers[3] + powers[4]
    return identity_mat + 2.0 * series + powers[5]


def chain_rule(grad_rot, powers):
    negated = [powers[degree] * (-1.0) ** (degree + 1) for degree in range(5)]
    partial_value = grad_rot
    running = 2.0 * grad_rot
    for degree in range(2, 7):
        partial_value = high_product(negated[0], partial_value) + high_product(
            grad_rot, negated[degree - 2]
        )
        weight_factor = 2.0 if degree < 6 else 1.0
        running = running + weight_factor * partial_value
    return running - jnp.swapaxes(running, -1, -2)


def body(activations, cotangent, base_weight, skew_param):
    full_skew = lax.all_gather(skew_param, "dp", axis=1, tiled=True)
    powers = power_list(full_skew)
    rotation = rotation_of(powers).astype(jnp.bfloat16)
    token_count = activations.shape[0]
    own_width = activations.shape[1]
    block_count = full_skew.shape[0]
    block_width = full_skew.shape[2]
    features = lax.psum_scatter(
        lax.dot_general(
            base_weight, cotangent, (((1,), (1,)), ((), ())), preferred_element_type=jnp.float32
        ),
        "outcol",
        scatter_dimension=0,
        tiled=True,
    )
    features = features.astype(jnp.bfloat16).reshape(block_count, block_width, token_count)
    grad_t = jnp.einsum(
        "bij,bjt->bit", rotation, features, preferred_element_type=jnp.float32
    ).astype(jnp.bfloat16)
    grad_acts = jnp.transpose(grad_t.reshape(own_width, token_count))
    grad_rot = jnp.einsum(
        "tbi,bjt->bij",
        activations.reshape(token_count, block_count, block_width),
        features,
        preferred_element_type=jnp.float32,
    )
    summed = lax.psum(grad_rot, "dp")
    grad_full = chain_rule(summed, powers)
    share_rows = block_width // lax.axis_size("dp")
    grad_skew = lax.dynamic_slice_in_dim(
        grad_full, lax.axis_index("dp") * share_rows, share_rows, 1
    )
    return (grad_acts, grad_skew)


def solution(mesh):
    return jax.shard_map(
        body,
        mesh=mesh,
        in_specs=(
            P("dp", ("inblk", "outcol")),
            P("dp", "outcol"),
            P("inblk", "outcol"),
            P(("inblk", "outcol"), "dp", None),
        ),
        out_specs=(P("dp", ("inblk", "outcol")), P(("inblk", "outcol"), "dp", None)),
        check_vma=False,
    )
```

profile of v0, /device:TPU:2, one launch (start us, length us, event | category | flops | bytes accessed | tf_op | source)
XLA Modules:
  0.0 434.7 jit_solution(13331793487568071938)
XLA Ops:
  7.2 0.0 copy-start
  7.2 0.0 reduce-scatter.2.cloned.1.call-start
  7.2 1.2 copy-done
  8.4 2.2 fusion.38
  10.6 0.0 copy-start.4
  10.6 0.0 reduce-scatter.2.cloned.1.call-update
  10.7 0.0 all-reduce.2.cloned.1.call-start
  10.7 0.6 copy-done.4
  11.4 92.4 %all_gather.3 = f32[2,256,256]{2,0,1:T(2,128)S(1)} all-gather(f32[2,8,256]{2,0,1:T(2,128)S(1)} %copy.12), channel_id=1, replica_groups=mesh['dp'=32,'inblk'=4,'outcol'=4] {'dp'}, dimensions={1}, use_global_device_ids=true | all-gather | bytes 540672 | tf_op jit(solution)/shard_map/all_gather | solution.py:40
  103.8 0.2 copy.13
  104.0 0.1 bitcast_subtract_fusion
  104.1 0.7 fusion.34
  104.7 0.7 fusion.35
  105.4 0.7 fusion.36
  106.1 1.5 fusion.37
  107.5 0.0 reduce-scatter.2.cloned.1.call-done
  107.5 0.0 copy-start.3
  107.5 1.0 convert_element_type.18
  108.5 0.0 copy-done.3
  108.5 1.1 convolution_bitcast_fusion
  109.6 0.0 all-reduce.2.cloned.1.call-update
  109.6 1.9 fusion.1
  111.6 0.2 convolution_convert_fusion
  111.8 0.8 copy.15
  112.5 306.2 %all-reduce.2.cloned.1.call-done = f32[2,256,256]{2,1,0:T(8,128)} async-done(((f32[2,256,256]{2,1,0:T(8,128)}), f32[2,256,256]{2,1,0:T(8,128)}) %all-reduce.2.cloned.1.call-update) | async-done | bytes 524304 | tf_op jit(solution)/shard_map/psum | solution.py:66
  418.7 0.0 copy-start.1
  418.7 1.8 fusion.13
  420.5 0.0 copy-done.1
  420.5 0.7 convolution_add_fusion.4
  421.2 0.7 fusion.10
  421.9 0.7 convolution_add_fusion.3
  422.6 0.7 fusion.8
  423.2 0.7 convolution_add_fusion.2
  423.9 0.7 fusion.6
  424.6 0.7 convolution_add_fusion.1
  425.2 0.0 copy-start.2
  425.3 0.7 fusion.4
  425.9 0.4 copy-done.2
  426.3 0.7 fusion
  427.0 0.2 copy.18
  427.2 0.6 dynamic-slice_subtract_fusion
  (2 shorter events, 0.0 us)
Async XLA Ops:
  7.2 1.2 copy-start
  7.2 100.3 %reduce-scatter.2.cloned.1.call-start = ((), (), s32[]{:S(2)}) async-start(), calls=%async_computation.1 | async-start | bytes 1310720 | tf_op jit(solution)/shard_map/reduce_scatter | solution.py:47
  10.6 0.7 copy-start.4
  10.7 408.1 %all-reduce.2.cloned.1.call-start = ((), (), s32[]{:S(2)}) async-start(), calls=%async_computation.2 | async-start | bytes 1048576 | tf_op jit(solution)/shard_map/psum | solution.py:66
  107.5 1.0 copy-start.3
  418.7 1.8 copy-start.1
  425.2 1.0 copy-start.2
Sparse Core Ops, SparseCore 0:
  10.9 31.1 reduce-scatter.1
  109.8 308.9 all-reduce.1
where the time goes:
time: 435 us
  waiting for transfers between devices  306 us (70%)
  blocking collectives  92.4 us (21%)
  matrix products  16.7 us (4%)
  between operations  14.2 us (3%)
    psum x1, waiting for transfers between devices, body(): summed = lax.psum(grad_rot, 'dp')  306 us
    all_gather x1, blocking collectives, body(): full_skew = lax.all_gather(skew_param, 'dp', axis=1, tiled=True)  92.4 us
    dot_general x15, matrix products, high_product(): return jnp.matmul(left, right, precision=lax.Precision.HIGHEST)  13.2 us
  transfers between devices with their start and end apart: 2, of which 1 were waited for; matrix products, arithmetic and copies ran while one was open for 2% of the time, Pallas kernels for 0%

commit v1 on v0

--- a/solution.py
+++ b/solution.py
@@ -63,7 +63,7 @@
         features,
         preferred_element_type=jnp.float32,
     )
-    summed = lax.psum(grad_rot, "dp")
+    summed = jnp.sum(lax.all_gather(grad_rot, "dp"), axis=0)
     grad_full = chain_rule(summed, powers)
     share_rows = block_width // lax.axis_size("dp")
     grad_skew = lax.dynamic_slice_in_dim(

time: 435 us -> 290 us (0.67)
  waiting for transfers between devices: 306 us -> 154 us
  other arithmetic: 1.71 us -> 8.09 us
    psum x1 -> x0, waiting for transfers between devices: 306 us -> none  [body(): summed = lax.psum(grad_rot, 'dp')]
    all_gather x0 -> x1, waiting for transfers between devices: none -> 124 us  [body(): summed = jnp.sum(lax.all_gather(grad_rot, 'dp'), axis=0)]
    reduce_scatter x1, waiting for transfers between devices: 0.01 us -> 30.3 us  [body(): lax.psum_scatter(lax.dot_general(base_weight, cotangent, (((1,), (1,)), (...]
    unnamed x0 -> x1, other arithmetic: none -> 6.89 us
  transfers between devices with their start and end apart: 2 -> 2, of which waited for: 1 -> 2; matrix products, arithmetic and copies ran while one was open for 2% -> 2% of each run, Pallas kernels for 0% -> 0%
where the time goes in v1:
time: 290 us; the launch traced here: 289 us
  waiting for transfers between devices  154 us (53%)
  blocking collectives  92.3 us (32%)
  matrix products  15.7 us (5%)
  between operations  14.3 us (5%)
  other arithmetic  8.09 us (3%)
  local copies, waits for them, and re-layouts  4.75 us (2%)
    all_gather x1, waiting for transfers between devices, body(): summed = jnp.sum(lax.all_gather(grad_rot, 'dp'), axis=0)  124 us
    all_gather x1, blocking collectives, body(): full_skew = lax.all_gather(skew_param, 'dp', axis=1, tiled=True)  92.3 us
    reduce_scatter x1, waiting for transfers between devices, body(): lax.psum_scatter(lax.dot_general(base_weight, cotangent, (((1,), (1,)), (...  30.3 us
    dot_general x15, matrix products, high_product(): return jnp.matmul(left, right, precision=lax.Precision.HIGHEST)  12.2 us
    unnamed x1, other arithmetic  6.89 us
  transfers between devices with their start and end apart: 2, of which 2 were waited for; matrix products, arithmetic and copies ran while one was open for 2% of the time, Pallas kernels for 0%

profile of v1, /device:TPU:2, one launch (start us, length us, event | category | flops | bytes accessed | tf_op | source)
XLA Modules:
  0.0 289.2 jit_solution(7865287874692615054)
XLA Ops:
  7.2 0.0 copy-start
  7.2 0.0 reduce-scatter.2.cloned.1.call-start
  7.2 1.2 copy-done
  8.4 2.2 fusion.38
  10.6 0.0 reduce-scatter.2.cloned.1.call-update
  10.7 0.0 all-gather.3.cloned.1.call-start
  10.7 30.3 %reduce-scatter.2.cloned.1.call-done = f32[512,128]{1,0:T(8,128)} async-done(((f32[2048,128]{1,0:T(8,128)}), f32[512,128]{1,0:T(8,128)}) %reduce-scatter.2.cloned.1.call-update) | async-done | bytes 262160 | tf_op jit(solution)/shard_map/reduce_scatter | solution.py:47
  41.0 1.0 convert_element_type.18
  42.0 1.1 convolution_bitcast_fusion
  43.1 1.0 copy.17
  44.1 0.0 all-gather.3.cloned.1.call-update
  44.1 0.7 copy.12
  44.9 92.3 %all_gather.9 = f32[2,256,256]{2,0,1:T(2,128)S(1)} all-gather(f32[2,8,256]{2,0,1:T(2,128)S(1)} %copy.12), channel_id=1, replica_groups=mesh['dp'=32,'inblk'=4,'outcol'=4] {'dp'}, dimensions={1}, use_global_device_ids=true | all-gather | bytes 540672 | tf_op jit(solution)/shard_map/all_gather | solution.py:40
  137.2 0.2 copy.13
  137.4 0.1 bitcast_subtract_fusion
  137.5 0.6 fusion.34
  138.2 0.0 copy-start.1
  138.2 0.7 fusion.35
  138.8 0.7 fusion.36
  139.5 0.7 fusion.37
  140.1 0.0 copy-done.1
  140.2 0.0 copy-start.2
  140.2 0.8 fusion.1
  141.0 0.0 copy-done.2
  141.0 0.2 convolution_convert_fusion
  141.2 0.8 copy.15
  142.0 123.6 %all-gather.3.cloned.1.call-done = f32[64,256,256]{2,1,0:T(8,128)} async-done(((f32[2,256,256]{2,1,0:T(8,128)}), f32[64,256,256]{2,1,0:T(8,128)}) %all-gather.3.cloned.1.call-update) | async-done | bytes 16777232 | tf_op jit(solution)/shard_map/all_gather | solution.py:66
  265.6 6.9 %reduce_sum.9 = f32[2,256,256]{2,1,0:T(8,128)S(1)} reduce(f32[32,2,256,256]{3,2,1,0:T(8,128)} %bitcast.40, f32[]{:T(128)} %constant.3.clone.1), dimensions={0}, to_apply=%region_1.0 | reduce | flops 4063232 | bytes 17301508
  272.5 0.7 fusion.13
  273.2 0.7 convolution_add_fusion.4
  273.9 0.7 fusion.10
  274.5 1.7 convolution_add_fusion.3
  276.2 0.7 fusion.8
  276.9 0.7 convolution_add_fusion.2
  277.6 0.7 fusion.6
  278.3 0.7 convolution_add_fusion.1
  278.9 0.7 fusion.4
  279.6 1.8 fusion
  281.4 0.1 copy.35
  281.5 0.1 dynamic-slice_subtract_fusion
  281.7 0.7 copy.27
  (2 shorter events, 0.0 us)
Async XLA Ops:
  7.2 1.2 copy-start
  7.2 33.8 %reduce-scatter.2.cloned.1.call-start = ((), (), s32[]{:S(2)}) async-start(), calls=%async_computation.1 | async-start | bytes 1310720 | tf_op jit(solution)/shard_map/reduce_scatter | solution.py:47
  10.7 255.0 %all-gather.3.cloned.1.call-start = ((), (), s32[]{:S(2)}) async-start(), calls=%async_computation.2 | async-start | bytes 17301504 | tf_op jit(solution)/shard_map/all_gather | solution.py:66
  138.2 2.0 copy-start.1
  140.2 0.8 copy-start.2
Sparse Core Ops, SparseCore 0:
  10.9 30.1 reduce-scatter.1
  44.7 220.8 all-gather.2

commit v2 on v0

--- a/solution.py
+++ b/solution.py
@@ -37,7 +37,9 @@
 
 
 def body(activations, cotangent, base_weight, skew_param):
-    full_skew = lax.all_gather(skew_param, "dp", axis=1, tiled=True)
+    full_skew = jnp.concatenate(
+        lax.all_to_all(jnp.stack([skew_param] * lax.axis_size("dp")), "dp", 0, 0), axis=1
+    )
     powers = power_list(full_skew)
     rotation = rotation_of(powers).astype(jnp.bfloat16)
     token_count = activations.shape[0]

time: 435 us -> 392 us (0.901)
  blocking collectives: 92.4 us -> 0 us
  waiting for transfers between devices: 306 us -> 340 us
  starting transfers between devices: 0.08 us -> 16.2 us
    all_gather x1 -> x0, blocking collectives: 92.4 us -> none  [body(): full_skew = lax.all_gather(skew_param, 'dp', axis=1, tiled=True)]
    all_to_all x0 -> x1, waiting for transfers between devices: none -> 17.2 us  [body(): lax.all_to_all(jnp.stack([skew_param] * lax.axis_size('dp')), 'dp', 0, 0)]
    all_to_all x0 -> x1, starting transfers between devices: none -> 16.1 us  [body(): lax.all_to_all(jnp.stack([skew_param] * lax.axis_size('dp')), 'dp', 0, 0)]
    psum x1, waiting for transfers between devices: 306 us -> 316 us  [body(): summed = lax.psum(grad_rot, 'dp')]
    reduce_scatter x1, waiting for transfers between devices: 0.01 us -> 7.47 us  [body(): lax.psum_scatter(lax.dot_general(base_weight, cotangent, (((1,), (1,)), (...]
  transfers between devices with their start and end apart: 2 -> 3, of which waited for: 1 -> 3; matrix products, arithmetic and copies ran while one was open for 2% -> 2% of each run, Pallas kernels for 0% -> 0%
where the time goes in v2:
time: 392 us; the launch traced here: 391 us
  waiting for transfers between devices  340 us (87%)
  starting transfers between devices  16.2 us (4%)
  matrix products  15.9 us (4%)
  between operations  14.3 us (4%)
    psum x1, waiting for transfers between devices, body(): summed = lax.psum(grad_rot, 'dp')  316 us
    all_to_all x1, waiting for transfers between devices, body(): lax.all_to_all(jnp.stack([skew_param] * lax.axis_size('dp')), 'dp', 0, 0)  17.2 us
    all_to_all x1, starting transfers between devices, body(): lax.all_to_all(jnp.stack([skew_param] * lax.axis_size('dp')), 'dp', 0, 0)  16.1 us
    dot_general x15, matrix products, high_product(): return jnp.matmul(left, right, precision=lax.Precision.HIGHEST)  13.2 us
  transfers between devices with their start and end apart: 3, of which 3 were waited for; matrix products, arithmetic and copies ran while one was open for 2% of the time, Pallas kernels for 0%

profile of v2, /device:TPU:2, one launch (start us, length us, event | category | flops | bytes accessed | tf_op | source)
XLA Modules:
  0.0 391.5 jit_solution(10305173627145851325)
XLA Ops:
  7.2 0.0 copy-start
  7.2 1.7 stack.2
  8.9 0.0 copy-start.4
  8.9 16.1 %all-to-all-start = ((f32[32,2,8,256]{3,2,1,0:T(8,128)}), f32[32,2,8,256]{3,2,1,0:T(8,128)S(1)}, u32[]{:S(2)}, u32[]{:S(2)}) async-start(f32[32,2,8,256]{3,2,1,0:T(8,128)} %stack.2), calls=%async_computation | async-start | bytes 1048576 | tf_op jit(solution)/shard_map/all_to_all | solution.py:41
  25.0 0.0 reduce-scatter.2.cloned.1.call-start
  25.0 0.0 copy-done
  25.0 0.0 copy-done.4
  25.0 1.4 fusion.38
  26.4 0.0 reduce-scatter.2.cloned.1.call-update
  26.5 0.0 all-reduce.2.cloned.1.call-start
  26.5 17.2 %all-to-all-done = f32[32,2,8,256]{3,2,1,0:T(8,128)S(1)} async-done(((f32[32,2,8,256]{3,2,1,0:T(8,128)}), f32[32,2,8,256]{3,2,1,0:T(8,128)S(1)}, u32[]{:S(2)}, u32[]{:S(2)}) %all-to-all-start) | async-done | bytes 524320 | tf_op jit(solution)/shard_map/all_to_all | solution.py:41
  43.8 0.2 copy.18
  44.0 0.1 bitcast_subtract_fusion
  44.1 0.7 fusion.34
  44.7 0.7 fusion.35
  45.4 0.7 fusion.36
  46.1 1.5 fusion.37
  47.5 7.5 %reduce-scatter.2.cloned.1.call-done = f32[512,128]{1,0:T(8,128)} async-done(((f32[2048,128]{1,0:T(8,128)}), f32[512,128]{1,0:T(8,128)}) %reduce-scatter.2.cloned.1.call-update) | async-done | bytes 262160 | tf_op jit(solution)/shard_map/reduce_scatter | solution.py:49
  55.0 0.0 copy-start.3
  55.0 1.0 convert_element_type.18
  56.0 0.0 copy-done.3
  56.0 1.1 convolution_bitcast_fusion
  57.1 0.0 all-reduce.2.cloned.1.call-update
  57.1 1.9 fusion.1
  59.0 0.2 convolution_convert_fusion
  59.3 0.8 copy.19
  60.0 315.5 %all-reduce.2.cloned.1.call-done = f32[2,256,256]{2,1,0:T(8,128)} async-done(((f32[2,256,256]{2,1,0:T(8,128)}), f32[2,256,256]{2,1,0:T(8,128)}) %all-reduce.2.cloned.1.call-update) | async-done | bytes 524304 | tf_op jit(solution)/shard_map/psum | solution.py:68
  375.5 0.0 copy-start.1
  375.5 1.8 fusion.13
  377.3 0.0 copy-done.1
  377.3 0.7 convolution_add_fusion.4
  378.0 0.7 fusion.10
  378.7 0.7 convolution_add_fusion.3
  379.3 0.7 fusion.8
  380.0 0.7 convolution_add_fusion.2
  380.7 0.7 fusion.6
  381.4 0.7 convolution_add_fusion.1
  382.0 0.0 copy-start.2
  382.0 0.7 fusion.4
  382.7 0.4 copy-done.2
  383.1 0.7 fusion
  383.8 0.2 copy.22
  384.0 0.6 dynamic-slice_subtract_fusion
  (2 shorter events, 0.1 us)
Async XLA Ops:
  7.2 17.9 %copy-start = (bf16[2048,256]{1,0:T(8,128)(2,1)S(1)}, bf16[2048,256]{1,0:T(8,128)(2,1)}, u32[]{:S(2)}) copy-start(bf16[2048,256]{1,0:T(8,128)(2,1)} %param.6) | copy-start | bytes 3145732
  8.9 16.2 %copy-start.4 = (bf16[128,256]{1,0:T(8,128)(2,1)S(1)}, bf16[128,256]{1,0:T(8,128)(2,1)}, u32[]{:S(2)}) copy-start(bf16[128,256]{1,0:T(8,128)(2,1)} %param.5) | copy-start | bytes 196612
  8.9 34.9 %all-to-all-start = ((f32[32,2,8,256]{3,2,1,0:T(8,128)}), f32[32,2,8,256]{3,2,1,0:T(8,128)S(1)}, u32[]{:S(2)}, u32[]{:S(2)}) async-start(f32[32,2,8,256]{3,2,1,0:T(8,128)} %stack.2), calls=%async_computation | async-start | bytes 1048576 | tf_op jit(solution)/shard_map/all_to_all | solution.py:41
  25.0 30.0 %reduce-scatter.2.cloned.1.call-start = ((), (), s32[]{:S(2)}) async-start(), calls=%async_computation.2 | async-start | bytes 1310720 | tf_op jit(solution)/shard_map/reduce_scatter | solution.py:49
  26.5 349.1 %all-reduce.2.cloned.1.call-start = ((), (), s32[]{:S(2)}) async-start(), calls=%async_computation.3 | async-start | bytes 1048576 | tf_op jit(solution)/shard_map/psum | solution.py:68
  55.0 1.0 copy-start.3
  375.5 1.8 copy-start.1
  382.0 1.0 copy-start.2
Sparse Core Ops, SparseCore 0:
  28.6 26.3 reduce-scatter.1
  58.2 317.3 all-reduce.1
